TPU v7x, 512 devices: a whole 4x8x8 slice. The times are simulated.
512 devices in a mesh: pole: 4 (over z_lo, core), row: 8 (over y), col: 16 (over x, z_hi).
Axes of the slice: x: 4, y: 8, z: 8 (z_hi: 4, z_lo: 2; z = z_hi * 2 + z_lo), core: 2. Of those that a mesh axis runs over, the one named last changes fastest.
Arguments:
- inverse: bfloat16 [12, 2, 6144, 6144], P('pole', None, 'col', 'row'), may hold values from -0.078125 to 0.078125
- lower: bfloat16 [12, 2, 6144, 512], P('pole', None, 'row', 'col'), may hold values from -6 to 6
- mask_tiles: int32 [16, 16], replicated, may hold values from 0 to 1, as said below
- pole_weight: float32 [12, 2], P('pole'), may hold values from -4 to 4
Outputs:
- panel: bfloat16 [12, 2, 6144, 512], P('pole', None, 'col', 'row')
- density: float32 [6144, 512], P(('col', 'pole'), 'row')
Inputs may be any that keep to these rules, and one draw needn't show every extreme that they name: `mask_tiles`: each tile row is either all ones or holds exactly one 1; of tile rows t and t + 8 exactly one is all ones.
All inputs are finite; a program needn't handle non-finite values.
Results may differ from a plain program's by a relative error of at most 0.017.
Values may be sent and summed in bfloat16 or wider, within the bound.
A program may use at most 128 MiB of HBM per device.

v0:
```python
import jax
import jax.numpy as jnp
from jax import lax
from jax.sharding import PartitionSpec as P

TILE = 384


def cut_along(array, dim, length):
    lengths = array.shape
    tiles = array.reshape(*lengths[:dim], length, lengths[dim] // length, *lengths[dim + 1 :])
    return jnp.moveaxis(tiles, dim, 0)


def sum_at_owner(array, axis, dim):
    tiles = cut_along(array, dim, lax.axis_size(axis))
    arrived = lax.all_to_all(tiles, axis, split_axis=0, concat_axis=0, tiled=True)
    return arrived.astype(jnp.float32).sum(axis=0)


def complex_product(block, factors):
    real_part = jnp.einsum(
        "prc,pcw->prw", block[:, 0], factors[:, 0], preferred_element_type=jnp.float32
    ) - jnp.einsum("prc,pcw->prw", block[:, 1], factors[:, 1], preferred_element_type=jnp.float32)
    imag_part = jnp.einsum(
        "prc,pcw->prw", block[:, 0], factors[:, 1], preferred_element_type=jnp.float32
    ) + jnp.einsum("prc,pcw->prw", block[:, 1], factors[:, 0], preferred_element_type=jnp.float32)
    return jnp.stack([real_part, imag_part], axis=1)


def body(inverse, lower, mask_tiles, pole_weight):
    full_lower = lax.all_gather(lower, "col", axis=3, tiled=True)
    rows_local = inverse.shape[2]
    cols_local = inverse.shape[3]
    row_tiles = rows_local // TILE
    col_tiles = cols_local // TILE
    half_tiles = col_tiles // 2
    split = half_tiles * TILE
    mine = lax.axis_index("col")
    first_col = lax.axis_index("row") * col_tiles

    def occupied(tiles, low, high):
        return jnp.sum(tiles[:, low:high]) > 0

    own = lax.dynamic_slice(mask_tiles, (mine * row_tiles, first_col), (row_tiles, col_tiles))
    keep = jnp.repeat(jnp.repeat(own, TILE, axis=0), TILE, axis=1).astype(jnp.bfloat16)
    kept = inverse * keep[None, None]
    left = kept[..., :split]
    right = kept[..., split:]
    lower_left = full_lower[:, :, :split]
    lower_right = full_lower[:, :, split:]
    empty = jnp.zeros((inverse.shape[0], 2, rows_local, full_lower.shape[3]), jnp.float32)

    def guarded(flag, block, factors):
        return lax.cond(flag, lambda: complex_product(block, factors), lambda: empty)

    own_left = occupied(own, 0, half_tiles)
    own_right = occupied(own, half_tiles, col_tiles)
    partial_value = guarded(own_left, left, lower_left)
    partial_value = partial_value + guarded(own_right, right, lower_right)
    summed = lax.psum_scatter(
        partial_value.astype(jnp.bfloat16), "row", scatter_dimension=3, tiled=True
    ).astype(jnp.float32)
    panel = (-summed).astype(jnp.bfloat16)
    values = panel.astype(jnp.float32)
    weighted = jnp.sum(
        pole_weight[:, 0, None, None] * values[:, 1] + pole_weight[:, 1, None, None] * values[:, 0],
        axis=0,
    )
    density = sum_at_owner(weighted.astype(jnp.bfloat16), "pole", 0)
    return (panel, density)


def solution(mesh):
    return jax.shard_map(
        body,
        mesh=mesh,
        in_specs=(
            P("pole", None, "col", "row"),
            P("pole", None, "row", "col"),
            P(),
            P("pole", None),
        ),
        out_specs=(P("pole", None, "col", "row"), P(("col", "pole"), "row")),
        check_vma=False,
    )
```

profile of v0, /device:TPU:1, one launch (start us, length us, event | category | flops | bytes accessed | tf_op | source)
XLA Modules:
  0.0 214.2 jit_solution(1438364237476678023)
XLA Ops:
  7.2 0.0 all-gather.2.cloned.1.call-start
  7.2 2.0 copy.12
  9.2 0.0 all-gather.2.cloned.1.call-update
  9.2 0.0 reduce-scatter.2.cloned.1.call-start
  9.3 0.8 convert_bitcast_fusion
  10.0 0.1 broadcast_in_dim.11
  10.1 0.6 fusion.41
  11.9 2.2 %copy_multiply_fusion = bf16[3,2,384,768]{3,2,0,1:T(8,128)(2,1)S(1)} fusion(bf16[3,2,384,768]{3,2,1,0:T(8,128)(2,1)} %param.8, bf16[768]{0:T(1024)(128)(2,1)S(1)} %convert_element_type.50), kind=kLoop, calls=%fused_computation.43 | loop fusion | flops 1769472 | bytes 7079424 | tf_op jit(solution)/shard_map/mul | solution.py:47
  14.2 91.8 %all-gather.2.cloned.1.call-done = bf16[3,2,768,512]{2,1,0,3:T(2,128)(2,1)} async-done(((bf16[3,2,768,32]{2,1,0,3:T(2,128)(2,1)}), bf16[3,2,768,512]{2,1,0,3:T(2,128)(2,1)}) %all-gather.2.cloned.1.call-update) | async-done | bytes 4718608 | tf_op jit(solution)/shard_map/all_gather | solution.py:32
  105.9 12.4 %copy.13 = bf16[3,2,768,512]{3,2,0,1:T(8,128)(2,1)} copy(bf16[3,2,768,512]{2,1,0,3:T(2,128)(2,1)} %all-gather.2.cloned.1.call-done) | data formatting | bytes 9437184 | tf_op jit(solution)/shard_map/cond | solution.py:55
  118.3 2.4 %conditional.3 = (f32[3,2,384,512]{2,3,1,0:T(8,128)}) conditional(s32[]{:T(128)} %bitcast.14, () %tuple.22, (bf16[3,2,384,768]{3,2,0,1:T(8,128)(2,1)S(1)}, bf16[3,2,768,512]{3,2,0,1:T(8,128)(2,1)}) %tuple.24), branch_computations={%region_2.0_spmd, %region_3.0_spmd} | conditional | flops 1814298624 | bytes 60162084 | solution.py:55
  118.3 2.4 %broadcast_in_dim.3.clone = f32[3,2,384,512]{2,3,1,0:T(8,128)} broadcast(f32[]{:T(128)} %constant.6.clone), dimensions={} | broadcast | bytes 4718596 | tf_op jit(solution)/shard_map/broadcast_in_dim | solution.py:52
  120.7 2.5 %conditional.2 = (f32[3,2,384,512]{2,3,1,0:T(8,128)}) conditional(s32[]{:T(128)} %bitcast.12, () %tuple.20, (bf16[3,2,384,768]{3,2,0,1:T(8,128)(2,1)S(1)}, bf16[3,2,768,512]{3,2,0,1:T(8,128)(2,1)}) %tuple.24), branch_computations={%region_0.0_spmd, %region_1.0_spmd} | conditional | flops 1814298624 | bytes 60162084 | solution.py:55
  120.7 2.5 %broadcast_in_dim.1.clone = f32[3,2,384,512]{2,3,1,0:T(8,128)} broadcast(f32[]{:T(128)} %constant.5.clone), dimensions={} | broadcast | bytes 4718596 | tf_op jit(solution)/shard_map/broadcast_in_dim | solution.py:52
  123.3 0.0 copy-start.2
  123.3 5.7 %add_convert_fusion = bf16[3,2,384,512]{2,3,1,0:T(8,128)(2,1)} fusion(f32[3,2,384,512]{2,3,1,0:T(8,128)} %get-tuple-element.28, f32[3,2,384,512]{2,3,1,0:T(8,128)} %get-tuple-element.29), kind=kLoop, calls=%fused_computation.42 | loop fusion | flops 2359296 | bytes 11796480 | tf_op jit(solution)/shard_map/convert_element_type | solution.py:62
  129.0 0.0 reduce-scatter.2.cloned.1.call-update
  129.0 0.0 copy-done.2
  129.0 64.6 %reduce-scatter.2.cloned.1.call-done = bf16[3,2,384,64]{2,3,1,0:T(8,128)(2,1)} async-done(((bf16[3,2,384,512]{2,3,1,0:T(8,128)(2,1)}), bf16[3,2,384,64]{2,3,1,0:T(8,128)(2,1)}) %reduce-scatter.2.cloned.1.call-update) | async-done | bytes 294928 | tf_op jit(solution)/shard_map/reduce_scatter | solution.py:61
  193.6 1.8 fusion.40
  195.4 0.1 fusion.38
  195.5 0.1 convert_element_type.58
  195.6 11.1 %all_to_all.5 = bf16[4,96,64]{1,2,0:T(8,128)(2,1)S(1)} all-to-all(bf16[4,96,64]{1,2,0:T(8,128)(2,1)S(1)} %copy.18), channel_id=1, replica_groups=mesh['pole'=4,'row'=8,'col'=16] {'pole'}, dimensions={0} | all-to-all | bytes 98304 | tf_op jit(solution)/shard_map/all_to_all | solution.py:17
  206.7 0.6 convert_reduce_fusion
  (3 shorter events, 0.0 us)
Async XLA Ops:
  7.2 98.8 %all-gather.2.cloned.1.call-start = ((), (), s32[]{:S(2)}) async-start(), calls=%async_computation.2 | async-start | bytes 5013504 | tf_op jit(solution)/shard_map/all_gather | solution.py:32
  9.2 184.4 %reduce-scatter.2.cloned.1.call-start = ((), (), s32[]{:S(2)}) async-start(), calls=%async_computation.3 | async-start | bytes 2654208 | tf_op jit(solution)/shard_map/reduce_scatter | solution.py:61
  123.3 5.7 %copy-start.2 = (f32[3,2]{0,1:T(2,128)S(1)}, f32[3,2]{0,1:T(2,128)}, u32[]{:S(2)}) copy-start(f32[3,2]{0,1:T(2,128)} %param.11) | copy-start | bytes 76
Sparse Core Ops, SparseCore 0:
  11.6 94.2 all-gather.1
  129.1 64.4 reduce-scatter.1
where the time goes:
time: 215 us; the launch traced here: 214 us
  waiting for transfers between devices  156 us (73%)
  local copies, waits for them, and re-layouts  20.1 us (9%)
  between operations  15.3 us (7%)
  other arithmetic  11.2 us (5%)
  blocking collectives  11.1 us (5%)
    all_gather x1, waiting for transfers between devices, body(): full_lower = lax.all_gather(lower, 'col', axis=3, tiled=True)  91.8 us
    reduce_scatter x1, waiting for transfers between devices, body(): lax.psum_scatter(partial_value.astype(jnp.bfloat16), 'row', scatter_dimen...  64.6 us
    cond x1, local copies, waits for them, and re-layouts, guarded(): lax.cond(flag, lambda: complex_product(block, factors), lambda: empty)  12.4 us
    all_to_all x1, blocking collectives, sum_at_owner(): lax.all_to_all(tiles, axis, split_axis=0, concat_axis=0, tiled=True)  11.1 us
    convert_element_type x1, other arithmetic, body(): partial_value.astype(jnp.bfloat16)  5.69 us
    broadcast_in_dim x2, local copies, waits for them, and re-layouts, body(): jnp.zeros((inverse.shape[0], 2, rows_local, full_lower.shape[3]), jnp.flo...  4.98 us
  transfers between devices with their start and end apart: 2, of which 2 were waited for; matrix products, arithmetic and copies ran while one was open for 2% of the time, Pallas kernels for 0%

commit v1 on v0

v1 whole, which is shorter than its diff:
```python
import functools

import jax
import jax.numpy as jnp
from jax import lax
from jax.experimental import pallas as pl
from jax.experimental.pallas import tpu as pltpu
from jax.sharding import PartitionSpec as P

MESH = pl.DeviceIdType.MESH
NX = 4
NZ = 4
NY = 8
NP = 4
KP = 3
TILE = 384
DEPTH = 768
WIDE = 32
OWN = 64
FULL = 512
PIECE = 96

ALL, LOW, HIGH = (0, 32), (0, 16), (16, 16)
TRANSFERS = (
    ((0, 0), ("z", 1), (0, -1), ALL),
    ((0, 0), ("z", -1), (0, 1), ALL),
    ((0, 0), ("x", 1), (-1, 0), ALL),
    ((0, 0), ("x", -1), (1, 0), ALL),
    ((0, -1), ("z", 1), (0, 2), LOW),
    ((0, 1), ("z", -1), (0, 2), HIGH),
    ((0, -1), ("x", 1), (-1, -1), ALL),
    ((0, -1), ("x", -1), (1, -1), ALL),
    ((0, 1), ("x", 1), (-1, 1), ALL),
    ((0, 1), ("x", -1), (1, 1), ALL),
    ((0, 2), ("x", 1), (-1, 2), ALL),
    ((0, 2), ("x", -1), (1, 2), ALL),
    ((-1, 0), ("x", 1), (2, 0), ALL),
    ((1, 2), ("x", -1), (2, 2), ALL),
    ((2, 0), ("z", 1), (2, -1), ALL),
    ((2, 0), ("z", -1), (2, 1), ALL),
)
NT = len(TRANSFERS)
NS = 7
NSUB = 2


def plan():
    steps = []
    for k in range(KP):
        steps += [("send", k, j) for j in (0, 1, 2, 3)]
    steps += [("own", 0, 0), ("weights", 0, 0)]
    for k in range(KP):
        ag = [
            [("get", k, 0)] + [("send", k, j) for j in (4, 6, 7)],
            [("get", k, 1)] + [("send", k, j) for j in (5, 8, 9)],
            [("get", k, 2), ("send", k, 12)],
            [("get", k, 4), ("get", k, 5)] + [("send", k, j) for j in (10, 11)],
            [("get", k, 12)] + [("send", k, j) for j in (14, 15)],
            [("get", k, 11), ("send", k, 13)],
            [("get", k, j) for j in (3, 6, 7, 8, 9, 10, 13, 14, 15)],
        ]
        rs = [[("reduce", k - 1, s)] for s in (1, 2, 3)] if k else []
        for i, group in enumerate(ag):
            steps += group
            if rs and i in (1, 3, 5):
                steps += rs.pop(0)
        if k:
            steps += [("finish", k - 1, 0)]
        steps += [("multiply", k, 0), ("reduce", k, 0)]
        if k + 1 < KP:
            steps += [("own", k + 1, 0), ("weights", k + 1, 0)]
    steps += [("reduce", KP - 1, s) for s in (1, 2, 3)]
    steps += [("finish", KP - 1, 0)]
    return steps


def kernel(
    inverse_ref, lower_ref, mask_ref, weight_ref, panel_ref, density_ref,
    block, factor, gathered, product, outgoing, incoming, pieces, pieces_out, pieces_in,
    block_sem, send_sem, recv_sem, rsend_sem, rrecv_sem, psend_sem, precv_sem,
):
    pole = lax.axis_index("pole")
    row = lax.axis_index("row")
    col = lax.axis_index("col")
    x, z = col // NZ, col % NZ

    def place(dx, dz):
        return lax.rem(x + NX + dx, NX) * NZ + lax.rem(z + NZ + dz, NZ)

    def along(step):
        axis, by = step
        return place(by, 0) if axis == "x" else place(0, by)

    def row_at(by):
        return lax.rem(row + NY + by, NY)

    def pole_at(by):
        return lax.rem(pole + by, NP)

    loads = [
        pltpu.make_async_copy(inverse_ref.at[k], block.at[k], block_sem.at[k]) for k in range(KP)
    ]
    for load in loads:
        load.start()

    barrier = pltpu.get_barrier_semaphore()
    for step in (("x", 1), ("x", -1), ("z", 1), ("z", -1)):
        pl.semaphore_signal(barrier, inc=1, device_id={"col": along(step)}, device_id_type=MESH)
    for by in (1, -1):
        pl.semaphore_signal(barrier, inc=1, device_id={"row": row_at(by)}, device_id_type=MESH)
    for by in (1, 2, 3):
        pl.semaphore_signal(barrier, inc=1, device_id={"pole": pole_at(by)}, device_id_type=MESH)
    pl.semaphore_wait(barrier, 9)

    def spot(k, chunk, rows):
        first = pl.multiple_of(place(*chunk) * WIDE + rows[0], 16)
        return gathered.at[k, :, pl.ds(first, rows[1]), :]

    def transfer(k, j, receiving):
        sent, step, got, rows = TRANSFERS[j]
        where = spot(k, got if receiving else sent, rows)
        source = where
        if not receiving and sent == (0, 0):
            source = lower_ref.at[k]
        return pltpu.make_async_remote_copy(
            src_ref=source,
            dst_ref=where,
            send_sem=send_sem.at[k, j],
            recv_sem=recv_sem.at[k, j],
            device_id={"col": along(step)},
            device_id_type=MESH,
        )

    def send(k, j):
        transfer(k, j, False).start()

    def get(k, j):
        transfer(k, j, True).wait_recv()

    def own(k, _):
        first = pl.multiple_of(place(0, 0) * WIDE, WIDE)
        gathered[k, :, pl.ds(first, WIDE), :] = lower_ref[k]

    def weights(k, _):
        loads[k].wait()
        left = mask_ref[col, 2 * row].astype(jnp.float32)
        right = mask_ref[col, 2 * row + 1].astype(jnp.float32)
        lane = lax.broadcasted_iota(jnp.int32, (1, DEPTH), 1)
        keep = jnp.where(lane < TILE, left, right)

        def some(i, carry):
            first = pl.multiple_of(i * 64, 64)
            re = block[k, 0, pl.ds(first, 64), :].astype(jnp.float32) * keep
            im = block[k, 1, pl.ds(first, 64), :].astype(jnp.float32) * keep
            minus_re = (-re).astype(jnp.bfloat16)
            factor[k, 0, pl.ds(first, 64), :DEPTH] = minus_re
            factor[k, 0, pl.ds(first, 64), DEPTH:] = im.astype(jnp.bfloat16)
            factor[k, 1, pl.ds(first, 64), :DEPTH] = (-im).astype(jnp.bfloat16)
            factor[k, 1, pl.ds(first, 64), DEPTH:] = minus_re
            return carry

        lax.fori_loop(0, TILE // 64, some, 0)

    def multiply(k, _):
        def some(i, carry):
            first = pl.multiple_of(i * 256, 256)
            both = jnp.concatenate(
                [gathered[k, 0, pl.ds(first, 256), :], gathered[k, 1, pl.ds(first, 256), :]], axis=1
            )
            for part in range(2):
                product[k, part, pl.ds(first, 256), :] = lax.dot_general(
                    both, factor[k, part], (((1,), (1,)), ((), ())), preferred_element_type=jnp.float32
                )
            return carry

        lax.fori_loop(0, FULL // 256, some, 0)

    def chains(k):
        turn = 1 if k % 2 == 0 else -1
        return ((0, turn, 4), (4, -turn, 3))

    def hop(k, slot, sub, to):
        return pltpu.make_async_remote_copy(
            src_ref=outgoing.at[k, slot, sub],
            dst_ref=incoming.at[k, slot, sub],
            send_sem=rsend_sem.at[k, slot, sub],
            recv_sem=rrecv_sem.at[k, slot, sub],
            device_id={"row": row_at(to)},
            device_id_type=MESH,
        )

    def mine(k, sub, owner):
        return product[k, sub, pl.ds(pl.multiple_of(owner * OWN, OWN), OWN), :]

    def reduce(k, s):
        for sub in range(NSUB):
            for base, turn, hops in chains(k):
                if s >= hops:
                    continue
                value = mine(k, sub, row_at(turn * (hops - s)))
                if s:
                    hop(k, base + s - 1, sub, turn).wait_recv()
                    value = value + incoming[k, base + s - 1, sub].astype(jnp.float32)
                outgoing[k, base + s, sub] = value.astype(jnp.bfloat16)
                hop(k, base + s, sub, turn).start()

    def finish(k, _):
        for sub in range(NSUB):
            value = mine(k, sub, row)
            for base, turn, hops in chains(k):
                hop(k, base + hops - 1, sub, turn).wait_recv()
                value = value + incoming[k, base + hops - 1, sub].astype(jnp.float32)
            panel_ref[k, sub] = value.astype(jnp.bfloat16)

    doing = dict(
        send=send, get=get, own=own, weights=weights, multiply=multiply, reduce=reduce, finish=finish
    )
    for what, k, index in plan():
        doing[what](k, index)

    weighted = jnp.zeros((OWN, TILE), jnp.float32)
    for k in range(KP):
        weighted = weighted + weight_ref[0, k] * panel_ref[k, 1].astype(jnp.float32)
        weighted = weighted + weight_ref[1, k] * panel_ref[k, 0].astype(jnp.float32)
    for q in range(NP):
        piece = weighted if q == 0 else pltpu.roll(weighted, TILE - PIECE * q, 1)
        pieces[q] = piece[:, :128]
        pieces_out[q] = piece[:, :128].astype(jnp.bfloat16)
    exchange = [
        pltpu.make_async_remote_copy(
            src_ref=pieces_out.at[pole_at(by)],
            dst_ref=pieces_in.at[by - 1],
            send_sem=psend_sem.at[by - 1],
            recv_sem=precv_sem.at[by - 1],
            device_id={"pole": pole_at(by)},
            device_id_type=MESH,
        )
        for by in range(1, NP)
    ]
    for copy in exchange:
        copy.start()
    total = pieces[pole]
    for by in range(1, NP):
        exchange[by - 1].wait_recv()
        total = total + pieces_in[by - 1].astype(jnp.float32)
    density_ref[...] = total[:, :PIECE]

    for copy in exchange:
        copy.wait_send()
    for k in range(KP):
        for j in range(NT):
            transfer(k, j, False).wait_send()
        for base, turn, hops in chains(k):
            for s in range(hops):
                for sub in range(NSUB):
                    hop(k, base + s, sub, turn).wait_send()


def body(inverse, lower, mask_tiles, pole_weight):
    vmem = pl.BlockSpec(memory_space=pltpu.VMEM)
    smem = pl.BlockSpec(memory_space=pltpu.SMEM)
    bf16, f32 = jnp.bfloat16, jnp.float32
    panel, density = pl.pallas_call(
        kernel,
        out_shape=(
            jax.ShapeDtypeStruct((KP, 2, OWN, TILE), bf16),
            jax.ShapeDtypeStruct((OWN, PIECE), f32),
        ),
        in_specs=[pl.BlockSpec(memory_space=pl.ANY), vmem, smem, smem],
        out_specs=(vmem, vmem),
        scratch_shapes=[
            pltpu.VMEM((KP, 2, TILE, DEPTH), bf16),
            pltpu.VMEM((KP, 2, TILE, 2 * DEPTH), bf16),
            pltpu.VMEM((KP, 2, FULL, DEPTH), bf16),
            pltpu.VMEM((KP, 2, FULL, TILE), f32),
            pltpu.VMEM((KP, NS, NSUB, OWN, TILE), bf16),
            pltpu.VMEM((KP, NS, NSUB, OWN, TILE), bf16),
            pltpu.VMEM((NP, OWN, 128), f32),
            pltpu.VMEM((NP, OWN, 128), bf16),
            pltpu.VMEM((NP - 1, OWN, 128), bf16),
            pltpu.SemaphoreType.DMA((KP,)),
            pltpu.SemaphoreType.DMA((KP, NT)),
            pltpu.SemaphoreType.DMA((KP, NT)),
            pltpu.SemaphoreType.DMA((KP, NS, NSUB)),
            pltpu.SemaphoreType.DMA((KP, NS, NSUB)),
            pltpu.SemaphoreType.DMA((NP - 1,)),
            pltpu.SemaphoreType.DMA((NP - 1,)),
        ],
        compiler_params=pltpu.CompilerParams(
            collective_id=0, has_side_effects=True, vmem_limit_bytes=56 * 1024 * 1024
        ),
        name="panel_update",
    )(inverse, jnp.swapaxes(lower, 2, 3), mask_tiles, jnp.swapaxes(pole_weight, 0, 1))
    return jnp.swapaxes(panel, 2, 3), jnp.swapaxes(density, 0, 1)


def solution(mesh):
    return jax.shard_map(
        body,
        mesh=mesh,
        in_specs=(
            P("pole", None, "col", "row"),
            P("pole", None, "row", "col"),
            P(),
            P("pole", None),
        ),
        out_specs=(P("pole", None, "col", "row"), P(("col", "pole"), "row")),
        check_vma=False,
    )
```

time: 215 us -> 99.7 us (0.46)
  waiting for transfers between devices: 156 us -> 0 us
  Pallas kernels: 0 us -> 95.8 us
  local copies, waits for them, and re-layouts: 20.1 us -> 3.08 us
  between operations: 15.3 us -> 0.64 us
  other arithmetic: 11.2 us -> 0 us
  blocking collectives: 11.1 us -> 0 us
    pallas_call x0 -> x1, Pallas kernels: none -> 95.8 us  [body(): pl.pallas_call(kernel, out_shape=(jax.ShapeDtypeStruct((KP, 2, OWN, TILE)...]
    all_gather x1 -> x0, waiting for transfers between devices: 91.8 us -> none  [body(): full_lower = lax.all_gather(lower, 'col', axis=3, tiled=True)]
    reduce_scatter x1 -> x0, waiting for transfers between devices: 64.6 us -> none  [body(): lax.psum_scatter(partial_value.astype(jnp.bfloat16), 'row', scatter_dimen...]
    cond x1 -> x0, local copies, waits for them, and re-layouts: 12.4 us -> none  [guarded(): lax.cond(flag, lambda: complex_product(block, factors), lambda: empty)]
    all_to_all x1 -> x0, blocking collectives: 11.1 us -> none  [sum_at_owner(): lax.all_to_all(tiles, axis, split_axis=0, concat_axis=0, tiled=True)]
    convert_element_type x3 -> x0, other arithmetic: 8.21 us -> none  [the longest x1 5.69 us: body(): partial_value.astype(jnp.bfloat16)]
    broadcast_in_dim x3 -> x0, local copies, waits for them, and re-layouts: 5.05 us -> none  [the longest x2 4.98 us: body(): jnp.zeros((inverse.shape[0], 2, rows_local, full_lower.shape[3]), jnp.flo...]
    mul x1 -> x0, other arithmetic: 2.24 us -> none  [body(): kept = inverse * keep[None, None]]
  transfers between devices with their start and end apart: 2 -> 0, of which waited for: 2 -> 0; matrix products, arithmetic and copies ran while one was open for 2% -> 0% of each run, Pallas kernels for 0% -> 0%
where the time goes in v1:
time: 99.7 us; the launch traced here: 99.5 us
  Pallas kernels  95.8 us (96%)
  local copies, waits for them, and re-layouts  3.08 us (3%)
    pallas_call x1, Pallas kernels, body(): pl.pallas_call(kernel, out_shape=(jax.ShapeDtypeStruct((KP, 2, OWN, TILE)...  95.8 us
    unnamed x2, local copies, waits for them, and re-layouts  3.08 us

profile of v1, /device:TPU:1, one launch (start us, length us, event | category | flops | bytes accessed | tf_op | source)
XLA Modules:
  0.0 99.5 jit_solution(5835540562992942402)
XLA Ops:
  0.6 95.8 %panel_update.1 = (bf16[3,2,64,384]{3,2,1,0:T(8,128)(2,1)}, f32[64,96]{1,0:T(8,128)}) custom-call(bf16[3,2,384,768]{3,2,1,0:T(8,128)(2,1)} %inverse_ref.1, bf16[3,2,32,768]{3,2,1,0:T(8,128)(2,1)} %bitcast.4, s32[16,16]{1,0:T(8,128)} %mask_ref.1, f32[2,3]{1,0:T(2,128)} %bitcast.7), custom_call_target="tpu_custom_call" | custom-call | tf_op jit(solution)/shard_map/panel_update/pallas_call | solution.py:263
  96.4 1.7 %copy.8 = bf16[3,2,384,64]{2,3,1,0:T(8,128)(2,1)} copy(bf16[3,2,384,64]{2,3,1,0:T(8,128)(2,1)} %bitcast.5) | data formatting | bytes 589824
  98.1 1.4 %copy.9 = f32[96,64]{0,1:T(8,128)} copy(f32[96,64]{0,1:T(8,128)} %bitcast.6) | data formatting | bytes 49152

commit v2 on v1

v2 whole, which is shorter than its diff:
```python
import jax
import jax.numpy as jnp
from jax import lax
from jax.experimental import pallas as pl
from jax.experimental.pallas import tpu as pltpu
from jax.sharding import PartitionSpec as P

MESH = pl.DeviceIdType.MESH
NX = 4
NZ = 4
NY = 8
NP = 4
KP = 3
TILE = 384
DEPTH = 768
WIDE = 32
OWN = 64
FULL = 512
PIECE = 96

ALL, LOW, HIGH = (0, 32), (0, 16), (16, 16)
TRANSFERS = (
    ((0, 0), ("z", 1), (0, -1), ALL),
    ((0, 0), ("z", -1), (0, 1), ALL),
    ((0, 0), ("x", 1), (-1, 0), ALL),
    ((0, 0), ("x", -1), (1, 0), ALL),
    ((0, -1), ("z", 1), (0, 2), LOW),
    ((0, 1), ("z", -1), (0, 2), HIGH),
    ((0, -1), ("x", 1), (-1, -1), ALL),
    ((0, -1), ("x", -1), (1, -1), ALL),
    ((0, 1), ("x", 1), (-1, 1), ALL),
    ((0, 1), ("x", -1), (1, 1), ALL),
    ((0, 2), ("x", 1), (-1, 2), ALL),
    ((0, 2), ("x", -1), (1, 2), ALL),
    ((-1, 0), ("x", 1), (2, 0), ALL),
    ((1, 2), ("x", -1), (2, 2), ALL),
    ((2, 0), ("z", 1), (2, -1), ALL),
    ((2, 0), ("z", -1), (2, 1), ALL),
)
NT = len(TRANSFERS)
NS = 7
SUBS = (2, 2, 4)
TILES = (2, 2, 4)

STEPS = (
    (0, 1, 2), (0, 0, 2), (0, 3, 3), (0, 0, 1), (0, 0, 0), (0, 0, 3), (0, 1, 1), (0, 5, 2), (0, 1, 0), (0, 1, 3),
    (1, 1, 2), (0, 2, 2), (0, 3, 2), (0, 1, 12), (0, 2, 1), (0, 4, 3), (0, 3, 0), (0, 2, 3), (0, 5, 3), (2, 0, 0),
    (1, 3, 3), (1, 0, 2), (0, 0, 12), (0, 3, 1), (0, 2, 0), (1, 0, 3), (1, 0, 1), (0, 0, 9), (1, 0, 0), (1, 5, 2),
    (0, 0, 6), (0, 0, 7), (1, 1, 3), (1, 2, 2), (0, 0, 8), (0, 0, 5), (0, 0, 4), (1, 4, 3), (1, 1, 1), (0, 1, 9),
    (1, 1, 0), (1, 3, 2), (0, 1, 6), (0, 1, 5), (0, 1, 4), (0, 1, 7), (1, 2, 3), (1, 1, 12), (0, 1, 8), (0, 1, 15),
    (0, 1, 14), (1, 5, 3), (1, 2, 1), (0, 2, 9), (1, 3, 0), (1, 0, 12), (0, 2, 8), (0, 3, 7), (1, 0, 9), (1, 0, 6),
    (0, 3, 6), (0, 0, 15), (0, 3, 4), (1, 0, 7), (1, 3, 1), (0, 3, 9), (1, 2, 0), (1, 0, 8), (0, 2, 6), (0, 2, 7),
    (0, 2, 4), (1, 1, 9), (1, 0, 5), (1, 0, 4), (1, 1, 6), (0, 0, 10), (0, 2, 5), (0, 0, 11), (0, 0, 14), (1, 1, 7),
    (1, 1, 5), (1, 1, 4), (1, 1, 8), (0, 1, 10), (0, 1, 11), (0, 3, 5), (1, 2, 9), (1, 2, 8), (0, 3, 12), (0, 4, 1),
    (0, 4, 0), (1, 3, 7), (1, 1, 15), (1, 1, 14), (1, 3, 6), (0, 4, 2), (1, 3, 9), (1, 3, 4), (1, 2, 6), (0, 2, 12),
    (0, 5, 1), (0, 5, 0), (1, 2, 7), (1, 0, 15), (1, 2, 4), (1, 0, 10), (0, 3, 8), (1, 0, 11), (0, 0, 13),
    (1, 2, 5), (0, 2, 11), (1, 1, 10), (0, 2, 10), (1, 1, 11), (0, 1, 13), (1, 3, 5), (0, 3, 11), (1, 0, 14),
    (1, 3, 12), (0, 3, 15), (0, 3, 10), (0, 3, 14), (1, 0, 13), (1, 4, 2), (0, 4, 12), (1, 2, 11), (0, 2, 13),
    (1, 4, 1), (0, 4, 5), (0, 4, 9), (1, 4, 0), (0, 4, 4), (0, 4, 7), (1, 2, 12), (0, 4, 6), (0, 2, 15), (0, 2, 14),
    (1, 1, 13), (0, 4, 8), (0, 5, 12), (3, 0, 0), (4, 0, 0), (4, 0, 32), (4, 0, 1), (4, 0, 33), (3, 0, 1),
    (2, 1, 0), (1, 3, 8), (1, 3, 11), (0, 3, 13), (1, 5, 1), (0, 5, 8), (0, 5, 5), (0, 5, 9), (1, 5, 0), (0, 5, 4),
    (0, 5, 6), (0, 5, 7), (1, 2, 10), (1, 2, 13), (1, 3, 10), (1, 4, 9), (1, 3, 15), (1, 3, 14), (1, 4, 12),
    (0, 4, 14), (0, 4, 15), (4, 0, 8), (4, 0, 40), (1, 4, 7), (1, 4, 5), (1, 4, 4), (0, 4, 11), (1, 4, 6),
    (0, 4, 10), (4, 0, 9), (4, 0, 41), (1, 4, 8), (1, 3, 13), (1, 2, 15), (1, 2, 14), (3, 1, 0), (4, 0, 16),
    (4, 0, 48), (4, 1, 0), (4, 1, 32), (4, 1, 1), (4, 0, 17), (4, 0, 49), (4, 1, 33), (3, 1, 1), (2, 2, 0),
    (1, 5, 12), (0, 5, 15), (0, 5, 14), (1, 5, 9), (1, 5, 5), (1, 5, 4), (0, 5, 10), (0, 5, 11), (1, 5, 8),
    (1, 5, 7), (1, 5, 6), (1, 4, 11), (0, 4, 13), (1, 4, 15), (1, 4, 14), (1, 4, 10), (4, 0, 24), (4, 1, 40),
    (4, 1, 8), (4, 0, 25), (4, 1, 9), (1, 5, 10), (1, 5, 11), (0, 5, 13), (4, 1, 41), (1, 4, 13), (5, 0, 0),
    (4, 1, 16), (1, 5, 15), (1, 5, 14), (4, 1, 48), (4, 1, 17), (1, 5, 13), (3, 2, 0), (4, 2, 0), (4, 2, 32),
    (4, 2, 1), (4, 2, 33), (4, 2, 2), (4, 2, 34), (4, 2, 3), (4, 2, 35), (4, 1, 24), (4, 1, 49), (5, 0, 1),
    (3, 2, 1), (4, 1, 25), (3, 2, 2), (4, 2, 8), (4, 2, 40), (4, 2, 9), (4, 2, 41), (4, 2, 10), (4, 2, 42),
    (3, 2, 3), (4, 2, 11), (4, 2, 43), (5, 1, 0), (4, 2, 16), (5, 1, 1), (4, 2, 17), (4, 2, 48), (4, 2, 18),
    (4, 2, 49), (4, 2, 19), (4, 2, 50), (4, 2, 24), (4, 2, 51), (4, 2, 25), (4, 2, 26), (4, 2, 27), (5, 2, 0),
    (5, 2, 1), (5, 2, 2), (5, 2, 3),
)


def kernel(
    inverse_ref, lower_ref, mask_ref, weight_ref, panel_ref, density_ref,
    block, factor, gathered, product, outgoing, incoming, panel, pieces, pieces_out, pieces_in,
    block_sem, own_sem, panel_sem, send_sem, recv_sem, rsend_sem, rrecv_sem, psend_sem, precv_sem,
):
    pole = lax.axis_index("pole")
    row = lax.axis_index("row")
    col = lax.axis_index("col")
    x, z = col // NZ, col % NZ

    def place(dx, dz):
        return lax.rem(x + NX + dx, NX) * NZ + lax.rem(z + NZ + dz, NZ)

    def along(step):
        axis, by = step
        return place(by, 0) if axis == "x" else place(0, by)

    def row_at(by):
        return lax.rem(row + NY + by, NY)

    def pole_at(by):
        return lax.rem(pole + by, NP)

    loads = [
        pltpu.make_async_copy(inverse_ref.at[k], block.at[k], block_sem.at[k]) for k in range(KP)
    ]
    first_own = pl.multiple_of(place(0, 0) * WIDE, WIDE)
    own = pltpu.make_async_copy(lower_ref, gathered.at[:, :, pl.ds(first_own, WIDE), :], own_sem)
    own.start()
    for load in loads:
        load.start()

    barrier = pltpu.get_barrier_semaphore()
    for step in (("x", 1), ("x", -1), ("z", 1), ("z", -1)):
        pl.semaphore_signal(barrier, inc=1, device_id={"col": along(step)}, device_id_type=MESH)
    for by in (1, -1):
        pl.semaphore_signal(barrier, inc=1, device_id={"row": row_at(by)}, device_id_type=MESH)
    for by in (1, 2, 3):
        pl.semaphore_signal(barrier, inc=1, device_id={"pole": pole_at(by)}, device_id_type=MESH)
    pl.semaphore_wait(barrier, 9)

    def spot(slab, chunk, rows):
        first = pl.multiple_of(place(*chunk) * WIDE + rows[0], 16)
        return gathered.at[slab // 2, slab % 2, pl.ds(first, rows[1]), :]

    def transfer(slab, j, receiving):
        sent, step, got, rows = TRANSFERS[j]
        where = spot(slab, got if receiving else sent, rows)
        source = where
        if not receiving and sent == (0, 0):
            source = lower_ref.at[slab // 2, slab % 2]
        return pltpu.make_async_remote_copy(
            src_ref=source,
            dst_ref=where,
            send_sem=send_sem.at[slab, j],
            recv_sem=recv_sem.at[slab, j],
            device_id={"col": along(step)},
            device_id_type=MESH,
        )

    def send(slab, j):
        transfer(slab, j, False).start()

    def get(slab, j):
        transfer(slab, j, True).wait_recv()

    def weights(k, _):
        loads[k].wait()
        if k == 0:
            own.wait()
        left = mask_ref[col, 2 * row].astype(jnp.float32)
        right = mask_ref[col, 2 * row + 1].astype(jnp.float32)
        lane = lax.broadcasted_iota(jnp.int32, (1, DEPTH), 1)
        keep = jnp.where(lane < TILE, left, right)

        def some(i, carry):
            first = pl.multiple_of(i * 64, 64)
            re = block[k, 0, pl.ds(first, 64), :].astype(jnp.float32) * keep
            im = block[k, 1, pl.ds(first, 64), :].astype(jnp.float32) * keep
            minus_re = (-re).astype(jnp.bfloat16)
            factor[k, 0, pl.ds(first, 64), :DEPTH] = minus_re
            factor[k, 0, pl.ds(first, 64), DEPTH:] = im.astype(jnp.bfloat16)
            factor[k, 1, pl.ds(first, 64), :DEPTH] = (-im).astype(jnp.bfloat16)
            factor[k, 1, pl.ds(first, 64), DEPTH:] = minus_re
            return carry

        lax.fori_loop(0, TILE // 64, some, 0)

    def turn_of(k):
        return 1 if k % 2 == 0 else -1

    def multiply(k, tile):
        turn = turn_of(k)
        places = range(tile * 4 // TILES[k], (tile + 1) * 4 // TILES[k])
        blocks = [(q, side) for q in places for side in range(2)]
        lines = []
        for q, side in blocks:
            owner = row_at(turn * (4 - q)) if side == 0 else row_at(-turn * (3 - q))
            rows = pl.ds(pl.multiple_of(owner * OWN, OWN), OWN)
            lines.append(jnp.concatenate([gathered[k, 0, rows, :], gathered[k, 1, rows, :]], axis=1))
        both = jnp.concatenate(lines, axis=0)
        for part in range(2):
            value = lax.dot_general(
                both, factor[k, part], (((1,), (1,)), ((), ())), preferred_element_type=jnp.float32
            )
            for i, (q, side) in enumerate(blocks):
                product[k, part, q, side] = value[i * OWN : (i + 1) * OWN]

    def part_of(k, sub):
        each = 2 * OWN // SUBS[k]
        per = SUBS[k] // 2
        return sub // per, pl.ds(sub % per * each, each)

    def hop_copy(k, slot, sub):
        part, rows = part_of(k, sub)
        to = turn_of(k) if slot < 4 else -turn_of(k)
        return pltpu.make_async_remote_copy(
            src_ref=outgoing.at[k, slot, part, rows, :],
            dst_ref=incoming.at[k, slot, part, rows, :],
            send_sem=rsend_sem.at[k, slot, sub],
            recv_sem=rrecv_sem.at[k, slot, sub],
            device_id={"row": row_at(to)},
            device_id_type=MESH,
        )

    def hop(k, index):
        slot, sub = index // 8, index % 8
        part, rows = part_of(k, sub)
        q, side = (slot, 0) if slot < 4 else (slot - 4, 1)
        value = product[k, part, q, side, rows, :]
        if q:
            hop_copy(k, slot - 1, sub).wait_recv()
            value = value + incoming[k, slot - 1, part, rows, :].astype(jnp.float32)
        outgoing[k, slot, part, rows, :] = value.astype(jnp.bfloat16)
        hop_copy(k, slot, sub).start()

    def finish(k, sub):
        part, rows = part_of(k, sub)
        value = product[k, part, 3, 1, rows, :]
        for slot in (3, 6):
            hop_copy(k, slot, sub).wait_recv()
            value = value + incoming[k, slot, part, rows, :].astype(jnp.float32)
        panel[k, part, rows, :] = value.astype(jnp.bfloat16)

    stores = [
        pltpu.make_async_copy(panel.at[k], panel_ref.at[k], panel_sem.at[k]) for k in range(KP)
    ]
    doing = (send, get, weights, multiply, hop, finish)
    left = list(SUBS)
    for what, k, index in STEPS:
        doing[what](k, index)
        if what == 5:
            left[k] -= 1
            if left[k] == 0:
                stores[k].start()

    weighted = jnp.zeros((OWN, TILE), jnp.float32)
    for k in range(KP):
        weighted = weighted + weight_ref[0, k] * panel[k, 1].astype(jnp.float32)
        weighted = weighted + weight_ref[1, k] * panel[k, 0].astype(jnp.float32)
    for q in range(NP):
        piece = weighted if q == 0 else pltpu.roll(weighted, TILE - PIECE * q, 1)
        pieces[q] = piece[:, :128]
        pieces_out[q] = piece[:, :128].astype(jnp.bfloat16)
    exchange = [
        pltpu.make_async_remote_copy(
            src_ref=pieces_out.at[pole_at(by)],
            dst_ref=pieces_in.at[by - 1],
            send_sem=psend_sem.at[by - 1],
            recv_sem=precv_sem.at[by - 1],
            device_id={"pole": pole_at(by)},
            device_id_type=MESH,
        )
        for by in range(1, NP)
    ]
    for copy in exchange:
        copy.start()

    for slab in range(2 * KP):
        for j in range(NT):
            transfer(slab, j, False).wait_send()
    for k in range(KP):
        stores[k].wait()
        for slot in range(NS):
            for sub in range(SUBS[k]):
                hop_copy(k, slot, sub).wait_send()

    total = pieces[pole]
    for copy in exchange:
        copy.wait()
    for by in range(1, NP):
        total = total + pieces_in[by - 1].astype(jnp.float32)
    density_ref[...] = total[:, :PIECE]


def body(inverse, lower, mask_tiles, pole_weight):
    anywhere = pl.BlockSpec(memory_space=pl.ANY)
    vmem = pl.BlockSpec(memory_space=pltpu.VMEM)
    smem = pl.BlockSpec(memory_space=pltpu.SMEM)
    bf16, f32 = jnp.bfloat16, jnp.float32
    panel, density = pl.pallas_call(
        kernel,
        out_shape=(
            jax.ShapeDtypeStruct((KP, 2, OWN, TILE), bf16),
            jax.ShapeDtypeStruct((OWN, PIECE), f32),
        ),
        in_specs=[anywhere, anywhere, smem, smem],
        out_specs=(anywhere, vmem),
        scratch_shapes=[
            pltpu.VMEM((KP, 2, TILE, DEPTH), bf16),
            pltpu.VMEM((KP, 2, TILE, 2 * DEPTH), bf16),
            pltpu.VMEM((KP, 2, FULL, DEPTH), bf16),
            pltpu.VMEM((KP, 2, 4, 2, OWN, TILE), f32),
            pltpu.VMEM((KP, NS, 2, OWN, TILE), bf16),
            pltpu.VMEM((KP, NS, 2, OWN, TILE), bf16),
            pltpu.VMEM((KP, 2, OWN, TILE), bf16),
            pltpu.VMEM((NP, OWN, 128), f32),
            pltpu.VMEM((NP, OWN, 128), bf16),
            pltpu.VMEM((NP - 1, OWN, 128), bf16),
            pltpu.SemaphoreType.DMA((KP,)),
            pltpu.SemaphoreType.DMA,
            pltpu.SemaphoreType.DMA((KP,)),
            pltpu.SemaphoreType.DMA((2 * KP, NT)),
            pltpu.SemaphoreType.DMA((2 * KP, NT)),
            pltpu.SemaphoreType.DMA((KP, NS, max(SUBS))),
            pltpu.SemaphoreType.DMA((KP, NS, max(SUBS))),
            pltpu.SemaphoreType.DMA((NP - 1,)),
            pltpu.SemaphoreType.DMA((NP - 1,)),
        ],
        compiler_params=pltpu.CompilerParams(
            collective_id=0, has_side_effects=True, vmem_limit_bytes=56 * 1024 * 1024
        ),
        name="panel_update",
    )(inverse, jnp.swapaxes(lower, 2, 3), mask_tiles, jnp.swapaxes(pole_weight, 0, 1))
    return jnp.swapaxes(panel, 2, 3), jnp.swapaxes(density, 0, 1)


def solution(mesh):
    return jax.shard_map(
        body,
        mesh=mesh,
        in_specs=(
            P("pole", None, "col", "row"),
            P("pole", None, "row", "col"),
            P(),
            P("pole", None),
        ),
        out_specs=(P("pole", None, "col", "row"), P(("col", "pole"), "row")),
        check_vma=False,
    )
```

time: 99.7 us -> 83.7 us (0.84)
  Pallas kernels: 95.8 us -> 79.7 us
    pallas_call x1, Pallas kernels: 95.8 us -> 79.7 us  [body(): pl.pallas_call(kernel, out_shape=(jax.ShapeDtypeStruct((KP, 2, OWN, TILE)...]
where the time goes in v2:
time: 83.7 us; the launch traced here: 83.4 us
  Pallas kernels  79.7 us (95%)
  local copies, waits for them, and re-layouts  3.08 us (4%)
    pallas_call x1, Pallas kernels, body(): pl.pallas_call(kernel, out_shape=(jax.ShapeDtypeStruct((KP, 2, OWN, TILE)...  79.7 us
    unnamed x2, local copies, waits for them, and re-layouts  3.08 us

profile of v2, /device:TPU:1, one launch (start us, length us, event | category | flops | bytes accessed | tf_op | source)
XLA Modules:
  0.0 83.4 jit_solution(16328748506014350883)
XLA Ops:
  0.6 79.7 %panel_update.1 = (bf16[3,2,64,384]{3,2,1,0:T(8,128)(2,1)}, f32[64,96]{1,0:T(8,128)}) custom-call(bf16[3,2,384,768]{3,2,1,0:T(8,128)(2,1)} %inverse_ref.1, bf16[3,2,32,768]{3,2,1,0:T(8,128)(2,1)} %bitcast.4, s32[16,16]{1,0:T(8,128)} %mask_ref.1, f32[2,3]{1,0:T(2,128)} %bitcast.7), custom_call_target="tpu_custom_call" | custom-call | tf_op jit(solution)/shard_map/panel_update/pallas_call | solution.py:278
  80.4 1.7 %copy.8 = bf16[3,2,384,64]{2,3,1,0:T(8,128)(2,1)} copy(bf16[3,2,384,64]{2,3,1,0:T(8,128)(2,1)} %bitcast.5) | data formatting | bytes 589824
  82.1 1.4 %copy.9 = f32[96,64]{0,1:T(8,128)} copy(f32[96,64]{0,1:T(8,128)} %bitcast.6) | data formatting | bytes 49152

commit v3 on v2

v3 whole, which is shorter than its diff:
```python
import jax
import jax.numpy as jnp
from jax import lax
from jax.experimental import pallas as pl
from jax.experimental.pallas import tpu as pltpu
from jax.sharding import PartitionSpec as P

MESH = pl.DeviceIdType.MESH
NX = 4
NZ = 4
NY = 8
NP = 4
KP = 3
TILE = 384
DEPTH = 768
WIDE = 32
OWN = 64
FULL = 512
PIECE = 96

ALL, LOW, HIGH = (0, 32), (0, 16), (16, 16)
TRANSFERS = (
    ((0, 0), ("z", 1), (0, -1), ALL),
    ((0, 0), ("z", -1), (0, 1), ALL),
    ((0, 0), ("x", 1), (-1, 0), ALL),
    ((0, 0), ("x", -1), (1, 0), ALL),
    ((0, -1), ("z", 1), (0, 2), LOW),
    ((0, 1), ("z", -1), (0, 2), HIGH),
    ((0, -1), ("x", 1), (-1, -1), ALL),
    ((0, -1), ("x", -1), (1, -1), ALL),
    ((0, 1), ("x", 1), (-1, 1), ALL),
    ((0, 1), ("x", -1), (1, 1), ALL),
    ((0, 2), ("x", 1), (-1, 2), ALL),
    ((0, 2), ("x", -1), (1, 2), ALL),
    ((-1, 0), ("x", 1), (2, 0), ALL),
    ((1, 2), ("x", -1), (2, 2), ALL),
    ((2, 0), ("z", 1), (2, -1), ALL),
    ((2, 0), ("z", -1), (2, 1), ALL),
)
NT = len(TRANSFERS)
NU = 2 * KP
HALF = OWN // 2
NS = 7
SUBS = (1, 1, 1, 1, 1, 2)

CHAIN = ((4, 1, ()), (3, 1, (0,)), (2, 1, (1,)), (1, 1, (2,)), (-3, -1, ()), (-2, -1, (4,)), (-1, -1, (5,)))
FAN = ((4, 2, ()), (3, 1, ()), (-3, -1, ()), (1, 1, ()), (-1, -1, ()), (2, 2, (0, 1)), (-2, -2, (2,)))
CHAIN_ENDS, FAN_ENDS = (3, 6), (3, 4, 5, 6)
LAST = NU - 1
OWNERS = ((4, 3, -3, 2, -2, 1, -1, 0),) * LAST + ((4, 3, -3, 1, -1, 2, -2, 0),)
TILES = (1, 1, 1, 1, 1, 2)

STEPS = (
    (0, 0, 2), (0, 0, 0), (0, 0, 1), (0, 1, 2), (0, 1, 1), (0, 2, 2), (0, 3, 3), (0, 0, 3), (0, 2, 3), (0, 1, 0),
    (1, 0, 2), (0, 0, 12), (0, 2, 1), (0, 3, 2), (0, 4, 3), (0, 5, 2), (0, 1, 3), (0, 3, 0), (0, 5, 3), (2, 0, 0),
    (0, 3, 1), (0, 2, 0), (1, 3, 3), (1, 1, 2), (0, 1, 12), (1, 0, 3), (1, 0, 0), (0, 0, 7), (1, 0, 1), (1, 2, 2),
    (0, 0, 6), (1, 2, 3), (0, 0, 9), (1, 0, 12), (0, 0, 5), (0, 0, 4), (0, 0, 15), (0, 0, 8), (0, 0, 14), (1, 4, 3),
    (1, 1, 0), (0, 1, 7), (1, 1, 1), (1, 3, 2), (0, 1, 8), (0, 1, 9), (1, 1, 3), (1, 5, 2), (0, 2, 12), (0, 1, 4),
    (0, 1, 5), (1, 5, 3), (1, 3, 0), (0, 3, 7), (1, 2, 1), (1, 1, 12), (0, 2, 9), (0, 1, 14), (0, 2, 5), (0, 2, 8),
    (1, 0, 7), (1, 0, 6), (0, 1, 6), (1, 0, 9), (0, 1, 15), (1, 2, 0), (0, 2, 7), (1, 3, 1), (1, 0, 8), (0, 3, 8),
    (0, 2, 4), (0, 3, 9), (1, 1, 7), (1, 0, 4), (1, 0, 5), (1, 1, 8), (0, 0, 10), (0, 3, 4), (0, 3, 5), (0, 0, 11),
    (1, 1, 9), (1, 2, 12), (0, 3, 6), (0, 2, 14), (0, 2, 15), (1, 3, 7), (1, 0, 14), (1, 0, 15), (1, 2, 8),
    (0, 3, 12), (1, 2, 9), (1, 1, 4), (1, 1, 5), (0, 1, 11), (1, 1, 6), (0, 1, 10), (0, 5, 0), (0, 5, 1), (1, 2, 7),
    (1, 2, 5), (1, 3, 8), (0, 4, 2), (1, 3, 9), (1, 1, 14), (1, 0, 10), (0, 5, 12), (0, 4, 0), (0, 4, 1),
    (1, 0, 11), (0, 0, 13), (1, 2, 4), (0, 2, 11), (1, 1, 15), (3, 0, 0), (0, 2, 10), (4, 0, 0), (4, 0, 32),
    (0, 2, 6), (1, 3, 6), (1, 1, 11), (0, 1, 13), (1, 3, 4), (1, 3, 5), (0, 3, 11), (1, 3, 12), (1, 1, 10),
    (0, 3, 15), (0, 3, 14), (0, 3, 10), (1, 2, 14), (1, 2, 15), (1, 0, 13), (1, 4, 2), (0, 4, 12), (1, 2, 11),
    (0, 2, 13), (4, 0, 8), (4, 0, 40), (1, 5, 12), (0, 5, 15), (0, 5, 14), (1, 5, 0), (0, 5, 7), (0, 5, 6),
    (1, 5, 1), (0, 5, 9), (1, 1, 13), (0, 5, 8), (3, 1, 0), (0, 5, 4), (0, 5, 5), (4, 1, 0), (4, 1, 32), (2, 1, 0),
    (1, 2, 10), (1, 3, 11), (0, 3, 13), (1, 2, 6), (1, 4, 0), (0, 4, 4), (0, 4, 6), (0, 4, 7), (1, 4, 1), (0, 4, 5),
    (0, 4, 8), (0, 4, 9), (1, 3, 10), (1, 2, 13), (4, 0, 16), (4, 0, 48), (1, 4, 12), (0, 4, 14), (0, 4, 15),
    (1, 5, 7), (1, 3, 14), (1, 3, 15), (3, 2, 0), (4, 2, 0), (4, 1, 8), (4, 1, 40), (4, 2, 32), (1, 5, 6),
    (1, 5, 9), (1, 5, 8), (1, 3, 13), (3, 3, 0), (4, 0, 24), (4, 3, 0), (4, 3, 32), (2, 2, 0), (1, 5, 14),
    (1, 5, 15), (1, 4, 6), (1, 4, 7), (1, 5, 4), (1, 5, 5), (0, 5, 11), (0, 5, 10), (1, 4, 8), (1, 4, 9), (1, 4, 4),
    (1, 4, 5), (0, 4, 11), (0, 4, 10), (4, 2, 8), (4, 1, 16), (4, 1, 48), (4, 2, 40), (1, 4, 14), (1, 4, 15),
    (3, 4, 0), (4, 3, 8), (4, 4, 0), (4, 4, 32), (5, 0, 0), (1, 5, 11), (0, 5, 13), (1, 5, 10), (4, 3, 40),
    (1, 4, 11), (0, 4, 13), (4, 1, 24), (1, 4, 10), (4, 2, 16), (4, 2, 48), (4, 3, 16), (4, 4, 8), (1, 5, 13),
    (4, 4, 40), (4, 3, 48), (1, 4, 13), (3, 5, 0), (4, 2, 24), (4, 5, 0), (4, 5, 1), (4, 5, 8), (4, 5, 9),
    (4, 5, 16), (4, 5, 17), (5, 1, 0), (3, 5, 1), (4, 4, 16), (4, 3, 24), (4, 5, 24), (4, 5, 25), (4, 5, 32),
    (4, 5, 33), (4, 4, 48), (5, 2, 0), (4, 5, 41), (4, 5, 48), (4, 5, 40), (4, 5, 49), (5, 3, 0), (4, 4, 24),
    (5, 5, 1), (5, 5, 0), (5, 4, 0),
)


def kernel(
    inverse_ref, lower_ref, mask_ref, weight_ref, panel_ref, density_ref,
    block, factor, gathered, product, outgoing, incoming, panel, pieces, pieces_out, pieces_in,
    block_sem, own_sem, panel_sem, send_sem, recv_sem, rsend_sem, rrecv_sem, psend_sem, precv_sem,
):
    pole = lax.axis_index("pole")
    row = lax.axis_index("row")
    col = lax.axis_index("col")
    x, z = col // NZ, col % NZ

    def place(dx, dz):
        return lax.rem(x + NX + dx, NX) * NZ + lax.rem(z + NZ + dz, NZ)

    def along(step):
        axis, by = step
        return place(by, 0) if axis == "x" else place(0, by)

    def row_at(by):
        return lax.rem(row + NY + by, NY)

    def pole_at(by):
        return lax.rem(pole + by, NP)

    loads = [
        pltpu.make_async_copy(inverse_ref.at[k], block.at[k], block_sem.at[k]) for k in range(KP)
    ]
    first_own = pl.multiple_of(place(0, 0) * WIDE, WIDE)
    own = pltpu.make_async_copy(lower_ref, gathered.at[:, :, pl.ds(first_own, WIDE), :], own_sem)
    own.start()
    for load in loads:
        load.start()

    barrier = pltpu.get_barrier_semaphore()
    for step in (("x", 1), ("x", -1), ("z", 1), ("z", -1)):
        pl.semaphore_signal(barrier, inc=1, device_id={"col": along(step)}, device_id_type=MESH)
    for by in (1, -1, 2, -2):
        pl.semaphore_signal(barrier, inc=1, device_id={"row": row_at(by)}, device_id_type=MESH)
    for by in (1, 2, 3):
        pl.semaphore_signal(barrier, inc=1, device_id={"pole": pole_at(by)}, device_id_type=MESH)
    pl.semaphore_wait(barrier, 11)

    def spot(slab, chunk, rows):
        first = pl.multiple_of(place(*chunk) * WIDE + rows[0], 16)
        return gathered.at[slab // 2, slab % 2, pl.ds(first, rows[1]), :]

    def transfer(slab, j, receiving):
        sent, step, got, rows = TRANSFERS[j]
        where = spot(slab, got if receiving else sent, rows)
        source = where
        if not receiving and sent == (0, 0):
            source = lower_ref.at[slab // 2, slab % 2]
        return pltpu.make_async_remote_copy(
            src_ref=source,
            dst_ref=where,
            send_sem=send_sem.at[slab, j],
            recv_sem=recv_sem.at[slab, j],
            device_id={"col": along(step)},
            device_id_type=MESH,
        )

    def send(slab, j):
        transfer(slab, j, False).start()

    def get(slab, j):
        transfer(slab, j, True).wait_recv()

    def weights(k, _):
        loads[k].wait()
        if k == 0:
            own.wait()
        left = mask_ref[col, 2 * row].astype(jnp.float32)
        right = mask_ref[col, 2 * row + 1].astype(jnp.float32)
        lane = lax.broadcasted_iota(jnp.int32, (1, DEPTH), 1)
        keep = jnp.where(lane < TILE, left, right)

        def some(i, carry):
            first = pl.multiple_of(i * 64, 64)
            re = block[k, 0, pl.ds(first, 64), :].astype(jnp.float32) * keep
            im = block[k, 1, pl.ds(first, 64), :].astype(jnp.float32) * keep
            minus_re = (-re).astype(jnp.bfloat16)
            factor[k, 0, pl.ds(first, 64), :DEPTH] = minus_re
            factor[k, 0, pl.ds(first, 64), DEPTH:] = im.astype(jnp.bfloat16)
            factor[k, 1, pl.ds(first, 64), :DEPTH] = (-im).astype(jnp.bfloat16)
            factor[k, 1, pl.ds(first, 64), DEPTH:] = minus_re
            return carry

        lax.fori_loop(0, TILE // 64, some, 0)

    def spread(unit, owner):
        odd = lax.rem(z + 1 + unit % 2, 2)
        return pl.ds(pl.multiple_of(row_at(owner) * OWN + odd * HALF, HALF), HALF)

    def multiply(unit, tile):
        k = unit // 2
        each = 8 // TILES[unit]
        owners = OWNERS[unit][tile * each : (tile + 1) * each]
        lines = []
        for owner in owners:
            rows = spread(unit, owner)
            lines.append(jnp.concatenate([gathered[k, 0, rows, :], gathered[k, 1, rows, :]], axis=1))
        both = jnp.concatenate(lines, axis=0)
        for part in range(2):
            value = lax.dot_general(
                both, factor[k, part], (((1,), (1,)), ((), ())), preferred_element_type=jnp.float32
            )
            for i, owner in enumerate(owners):
                product[unit, part, owner % 8] = value[i * HALF : (i + 1) * HALF]

    def way(unit, slot, sub):
        turn = 1 if (sub if unit == LAST else unit) % 2 == 0 else -1
        owner, step, needs = (FAN if unit == LAST else CHAIN)[slot]
        return turn * owner % 8, turn * step, needs

    def parts_of(unit, sub):
        return slice(None) if SUBS[unit] == 1 else slice(sub, sub + 1)

    def hop_copy(unit, slot, sub):
        parts = pl.ds(0, 2) if SUBS[unit] == 1 else pl.ds(sub, 1)
        return pltpu.make_async_remote_copy(
            src_ref=outgoing.at[unit, slot, parts],
            dst_ref=incoming.at[unit, slot, parts],
            send_sem=rsend_sem.at[unit, slot, sub],
            recv_sem=rrecv_sem.at[unit, slot, sub],
            device_id={"row": row_at(way(unit, slot, sub)[1])},
            device_id_type=MESH,
        )

    def summed(unit, owner, slots, sub):
        parts = parts_of(unit, sub)
        value = product[unit, parts, owner]
        for slot in slots:
            hop_copy(unit, slot, sub).wait_recv()
            value = value + incoming[unit, slot, parts].astype(jnp.float32)
        return value.astype(jnp.bfloat16)

    def hop(unit, index):
        slot, sub = index // 8, index % 8
        owner, _, needs = way(unit, slot, sub)
        outgoing[unit, slot, parts_of(unit, sub)] = summed(unit, owner, needs, sub)
        hop_copy(unit, slot, sub).start()

    def finish(unit, sub):
        odd = lax.rem(z + 1 + unit % 2, 2)
        rows = pl.ds(pl.multiple_of(odd * HALF, HALF), HALF)
        ends = FAN_ENDS if unit == LAST else CHAIN_ENDS
        panel[unit // 2, parts_of(unit, sub), rows, :] = summed(unit, 0, ends, sub)

    stores = [
        pltpu.make_async_copy(panel.at[k], panel_ref.at[k], panel_sem.at[k]) for k in range(KP)
    ]
    doing = (send, get, weights, multiply, hop, finish)
    left = [SUBS[2 * k] + SUBS[2 * k + 1] for k in range(KP)]
    for what, which, index in STEPS:
        doing[what](which, index)
        if what == 5:
            left[which // 2] -= 1
            if left[which // 2] == 0:
                stores[which // 2].start()

    weighted = jnp.zeros((OWN, TILE), jnp.float32)
    for k in range(KP):
        weighted = weighted + weight_ref[0, k] * panel[k, 1].astype(jnp.float32)
        weighted = weighted + weight_ref[1, k] * panel[k, 0].astype(jnp.float32)
    for q in range(NP):
        piece = weighted if q == 0 else pltpu.roll(weighted, TILE - PIECE * q, 1)
        pieces[q] = piece[:, :128]
        pieces_out[q] = piece[:, :128].astype(jnp.bfloat16)
    exchange = [
        pltpu.make_async_remote_copy(
            src_ref=pieces_out.at[pole_at(by)],
            dst_ref=pieces_in.at[by - 1],
            send_sem=psend_sem.at[by - 1],
            recv_sem=precv_sem.at[by - 1],
            device_id={"pole": pole_at(by)},
            device_id_type=MESH,
        )
        for by in range(1, NP)
    ]
    for copy in exchange:
        copy.start()

    for slab in range(2 * KP):
        for j in range(NT):
            transfer(slab, j, False).wait_send()
    for store in stores:
        store.wait()
    for unit in range(NU):
        for slot in range(NS):
            for sub in range(SUBS[unit]):
                hop_copy(unit, slot, sub).wait_send()

    total = pieces[pole]
    for copy in exchange:
        copy.wait()
    for by in range(1, NP):
        total = total + pieces_in[by - 1].astype(jnp.float32)
    density_ref[...] = total[:, :PIECE]


def body(inverse, lower, mask_tiles, pole_weight):
    anywhere = pl.BlockSpec(memory_space=pl.ANY)
    vmem = pl.BlockSpec(memory_space=pltpu.VMEM)
    smem = pl.BlockSpec(memory_space=pltpu.SMEM)
    bf16, f32 = jnp.bfloat16, jnp.float32
    panel, density = pl.pallas_call(
        kernel,
        out_shape=(
            jax.ShapeDtypeStruct((KP, 2, OWN, TILE), bf16),
            jax.ShapeDtypeStruct((OWN, PIECE), f32),
        ),
        in_specs=[anywhere, anywhere, smem, smem],
        out_specs=(anywhere, vmem),
        scratch_shapes=[
            pltpu.VMEM((KP, 2, TILE, DEPTH), bf16),
            pltpu.VMEM((KP, 2, TILE, 2 * DEPTH), bf16),
            pltpu.VMEM((KP, 2, FULL, DEPTH), bf16),
            pltpu.VMEM((NU, 2, NY, HALF, TILE), f32),
            pltpu.VMEM((NU, NS, 2, HALF, TILE), bf16),
            pltpu.VMEM((NU, NS, 2, HALF, TILE), bf16),
            pltpu.VMEM((KP, 2, OWN, TILE), bf16),
            pltpu.VMEM((NP, OWN, 128), f32),
            pltpu.VMEM((NP, OWN, 128), bf16),
            pltpu.VMEM((NP - 1, OWN, 128), bf16),
            pltpu.SemaphoreType.DMA((KP,)),
            pltpu.SemaphoreType.DMA,
            pltpu.SemaphoreType.DMA((KP,)),
            pltpu.SemaphoreType.DMA((2 * KP, NT)),
            pltpu.SemaphoreType.DMA((2 * KP, NT)),
            pltpu.SemaphoreType.DMA((NU, NS, max(SUBS))),
            pltpu.SemaphoreType.DMA((NU, NS, max(SUBS))),
            pltpu.SemaphoreType.DMA((NP - 1,)),
            pltpu.SemaphoreType.DMA((NP - 1,)),
        ],
        compiler_params=pltpu.CompilerParams(
            collective_id=0, has_side_effects=True, vmem_limit_bytes=56 * 1024 * 1024
        ),
        name="panel_update",
    )(inverse, jnp.swapaxes(lower, 2, 3), mask_tiles, jnp.swapaxes(pole_weight, 0, 1))
    return jnp.swapaxes(panel, 2, 3), jnp.swapaxes(density, 0, 1)


def solution(mesh):
    return jax.shard_map(
        body,
        mesh=mesh,
        in_specs=(
            P("pole", None, "col", "row"),
            P("pole", None, "row", "col"),
            P(),
            P("pole", None),
        ),
        out_specs=(P("pole", None, "col", "row"), P(("col", "pole"), "row")),
        check_vma=False,
    )
```

time: 83.7 us -> 80.4 us (0.961)
  Pallas kernels: 79.7 us -> 76.4 us
    pallas_call x1, Pallas kernels: 79.7 us -> 76.4 us  [body(): pl.pallas_call(kernel, out_shape=(jax.ShapeDtypeStruct((KP, 2, OWN, TILE)...]
where the time goes in v3:
time: 80.4 us; the launch traced here: 80.1 us
  Pallas kernels  76.4 us (95%)
  local copies, waits for them, and re-layouts  3.08 us (4%)
    pallas_call x1, Pallas kernels, body(): pl.pallas_call(kernel, out_shape=(jax.ShapeDtypeStruct((KP, 2, OWN, TILE)...  76.4 us
    unnamed x2, local copies, waits for them, and re-layouts  3.08 us

profile of v3, /device:TPU:1, one launch (start us, length us, event | category | flops | bytes accessed | tf_op | source)
XLA Modules:
  0.0 80.1 jit_solution(877638180675424231)
XLA Ops:
  0.6 76.4 %panel_update.1 = (bf16[3,2,64,384]{3,2,1,0:T(8,128)(2,1)}, f32[64,96]{1,0:T(8,128)}) custom-call(bf16[3,2,384,768]{3,2,1,0:T(8,128)(2,1)} %inverse_ref.1, bf16[3,2,32,768]{3,2,1,0:T(8,128)(2,1)} %bitcast.4, s32[16,16]{1,0:T(8,128)} %mask_ref.1, f32[2,3]{1,0:T(2,128)} %bitcast.7), custom_call_target="tpu_custom_call" | custom-call | tf_op jit(solution)/shard_map/panel_update/pallas_call | solution.py:289
  77.1 1.7 %copy.8 = bf16[3,2,384,64]{2,3,1,0:T(8,128)(2,1)} copy(bf16[3,2,384,64]{2,3,1,0:T(8,128)(2,1)} %bitcast.5) | data formatting | bytes 589824
  78.8 1.4 %copy.9 = f32[96,64]{0,1:T(8,128)} copy(f32[96,64]{0,1:T(8,128)} %bitcast.6) | data formatting | bytes 49152

commit v4 on v3

--- a/solution.py
+++ b/solution.py
@@ -47,38 +47,36 @@
 FAN = ((4, 2, ()), (3, 1, ()), (-3, -1, ()), (1, 1, ()), (-1, -1, ()), (2, 2, (0, 1)), (-2, -2, (2,)))
 CHAIN_ENDS, FAN_ENDS = (3, 6), (3, 4, 5, 6)
 LAST = NU - 1
-OWNERS = ((4, 3, -3, 2, -2, 1, -1, 0),) * LAST + ((4, 3, -3, 1, -1, 2, -2, 0),)
-TILES = (1, 1, 1, 1, 1, 2)
 
 STEPS = (
-    (0, 0, 2), (0, 0, 0), (0, 0, 1), (0, 1, 2), (0, 1, 1), (0, 2, 2), (0, 3, 3), (0, 0, 3), (0, 2, 3), (0, 1, 0),
-    (1, 0, 2), (0, 0, 12), (0, 2, 1), (0, 3, 2), (0, 4, 3), (0, 5, 2), (0, 1, 3), (0, 3, 0), (0, 5, 3), (2, 0, 0),
-    (0, 3, 1), (0, 2, 0), (1, 3, 3), (1, 1, 2), (0, 1, 12), (1, 0, 3), (1, 0, 0), (0, 0, 7), (1, 0, 1), (1, 2, 2),
-    (0, 0, 6), (1, 2, 3), (0, 0, 9), (1, 0, 12), (0, 0, 5), (0, 0, 4), (0, 0, 15), (0, 0, 8), (0, 0, 14), (1, 4, 3),
-    (1, 1, 0), (0, 1, 7), (1, 1, 1), (1, 3, 2), (0, 1, 8), (0, 1, 9), (1, 1, 3), (1, 5, 2), (0, 2, 12), (0, 1, 4),
-    (0, 1, 5), (1, 5, 3), (1, 3, 0), (0, 3, 7), (1, 2, 1), (1, 1, 12), (0, 2, 9), (0, 1, 14), (0, 2, 5), (0, 2, 8),
-    (1, 0, 7), (1, 0, 6), (0, 1, 6), (1, 0, 9), (0, 1, 15), (1, 2, 0), (0, 2, 7), (1, 3, 1), (1, 0, 8), (0, 3, 8),
-    (0, 2, 4), (0, 3, 9), (1, 1, 7), (1, 0, 4), (1, 0, 5), (1, 1, 8), (0, 0, 10), (0, 3, 4), (0, 3, 5), (0, 0, 11),
-    (1, 1, 9), (1, 2, 12), (0, 3, 6), (0, 2, 14), (0, 2, 15), (1, 3, 7), (1, 0, 14), (1, 0, 15), (1, 2, 8),
-    (0, 3, 12), (1, 2, 9), (1, 1, 4), (1, 1, 5), (0, 1, 11), (1, 1, 6), (0, 1, 10), (0, 5, 0), (0, 5, 1), (1, 2, 7),
-    (1, 2, 5), (1, 3, 8), (0, 4, 2), (1, 3, 9), (1, 1, 14), (1, 0, 10), (0, 5, 12), (0, 4, 0), (0, 4, 1),
-    (1, 0, 11), (0, 0, 13), (1, 2, 4), (0, 2, 11), (1, 1, 15), (3, 0, 0), (0, 2, 10), (4, 0, 0), (4, 0, 32),
-    (0, 2, 6), (1, 3, 6), (1, 1, 11), (0, 1, 13), (1, 3, 4), (1, 3, 5), (0, 3, 11), (1, 3, 12), (1, 1, 10),
-    (0, 3, 15), (0, 3, 14), (0, 3, 10), (1, 2, 14), (1, 2, 15), (1, 0, 13), (1, 4, 2), (0, 4, 12), (1, 2, 11),
-    (0, 2, 13), (4, 0, 8), (4, 0, 40), (1, 5, 12), (0, 5, 15), (0, 5, 14), (1, 5, 0), (0, 5, 7), (0, 5, 6),
-    (1, 5, 1), (0, 5, 9), (1, 1, 13), (0, 5, 8), (3, 1, 0), (0, 5, 4), (0, 5, 5), (4, 1, 0), (4, 1, 32), (2, 1, 0),
-    (1, 2, 10), (1, 3, 11), (0, 3, 13), (1, 2, 6), (1, 4, 0), (0, 4, 4), (0, 4, 6), (0, 4, 7), (1, 4, 1), (0, 4, 5),
-    (0, 4, 8), (0, 4, 9), (1, 3, 10), (1, 2, 13), (4, 0, 16), (4, 0, 48), (1, 4, 12), (0, 4, 14), (0, 4, 15),
-    (1, 5, 7), (1, 3, 14), (1, 3, 15), (3, 2, 0), (4, 2, 0), (4, 1, 8), (4, 1, 40), (4, 2, 32), (1, 5, 6),
-    (1, 5, 9), (1, 5, 8), (1, 3, 13), (3, 3, 0), (4, 0, 24), (4, 3, 0), (4, 3, 32), (2, 2, 0), (1, 5, 14),
-    (1, 5, 15), (1, 4, 6), (1, 4, 7), (1, 5, 4), (1, 5, 5), (0, 5, 11), (0, 5, 10), (1, 4, 8), (1, 4, 9), (1, 4, 4),
-    (1, 4, 5), (0, 4, 11), (0, 4, 10), (4, 2, 8), (4, 1, 16), (4, 1, 48), (4, 2, 40), (1, 4, 14), (1, 4, 15),
-    (3, 4, 0), (4, 3, 8), (4, 4, 0), (4, 4, 32), (5, 0, 0), (1, 5, 11), (0, 5, 13), (1, 5, 10), (4, 3, 40),
-    (1, 4, 11), (0, 4, 13), (4, 1, 24), (1, 4, 10), (4, 2, 16), (4, 2, 48), (4, 3, 16), (4, 4, 8), (1, 5, 13),
-    (4, 4, 40), (4, 3, 48), (1, 4, 13), (3, 5, 0), (4, 2, 24), (4, 5, 0), (4, 5, 1), (4, 5, 8), (4, 5, 9),
-    (4, 5, 16), (4, 5, 17), (5, 1, 0), (3, 5, 1), (4, 4, 16), (4, 3, 24), (4, 5, 24), (4, 5, 25), (4, 5, 32),
-    (4, 5, 33), (4, 4, 48), (5, 2, 0), (4, 5, 41), (4, 5, 48), (4, 5, 40), (4, 5, 49), (5, 3, 0), (4, 4, 24),
-    (5, 5, 1), (5, 5, 0), (5, 4, 0),
+    (0, 0, 2), (0, 1, 1), (0, 0, 0), (0, 0, 3), (0, 0, 1), (0, 1, 3), (0, 1, 2), (0, 1, 0), (0, 4, 3), (0, 5, 2),
+    (1, 0, 2), (0, 0, 12), (0, 2, 1), (0, 2, 3), (0, 2, 0), (0, 2, 2), (0, 3, 3), (0, 3, 2), (0, 5, 3), (2, 0, 0),
+    (0, 3, 1), (0, 3, 0), (1, 0, 3), (1, 1, 2), (0, 1, 12), (1, 1, 3), (1, 1, 1), (0, 1, 9), (1, 0, 0), (1, 5, 2),
+    (0, 0, 7), (0, 1, 8), (1, 4, 3), (1, 0, 12), (0, 0, 15), (0, 0, 14), (0, 0, 6), (1, 2, 3), (1, 0, 1), (0, 0, 9),
+    (1, 1, 0), (1, 2, 2), (0, 1, 5), (0, 1, 7), (0, 0, 8), (0, 1, 4), (1, 3, 3), (1, 3, 2), (0, 0, 5), (0, 2, 12),
+    (0, 0, 4), (1, 5, 3), (1, 2, 1), (0, 2, 9), (1, 2, 0), (1, 1, 12), (0, 1, 15), (0, 2, 7), (0, 1, 14), (0, 1, 6),
+    (1, 1, 9), (1, 1, 8), (0, 2, 8), (1, 0, 7), (1, 3, 1), (0, 3, 9), (1, 3, 0), (1, 0, 6), (0, 3, 8), (0, 2, 5),
+    (0, 2, 4), (0, 3, 7), (1, 0, 9), (1, 0, 8), (0, 3, 5), (0, 3, 4), (0, 3, 12), (1, 1, 7), (1, 0, 15), (1, 0, 14),
+    (1, 2, 12), (0, 2, 15), (0, 2, 14), (0, 2, 6), (1, 2, 9), (1, 1, 5), (1, 1, 4), (0, 1, 11), (1, 1, 6),
+    (0, 1, 10), (1, 2, 7), (1, 0, 5), (1, 0, 4), (0, 0, 11), (1, 2, 8), (0, 0, 10), (0, 5, 1), (0, 4, 0), (1, 3, 9),
+    (1, 3, 8), (0, 4, 2), (1, 3, 7), (1, 1, 15), (1, 1, 14), (3, 0, 0), (0, 5, 12), (3, 0, 1), (0, 4, 1), (0, 5, 0),
+    (4, 0, 0), (0, 3, 6), (4, 0, 32), (1, 3, 12), (1, 1, 11), (0, 1, 13), (1, 2, 5), (1, 2, 4), (0, 2, 11),
+    (1, 2, 6), (1, 0, 11), (0, 0, 13), (1, 3, 5), (1, 3, 4), (1, 1, 10), (0, 3, 15), (0, 3, 11), (0, 3, 14),
+    (0, 2, 10), (1, 0, 10), (0, 3, 10), (1, 2, 15), (1, 2, 14), (4, 0, 8), (1, 4, 2), (0, 4, 12), (4, 0, 40),
+    (1, 1, 13), (1, 5, 12), (0, 5, 15), (0, 5, 14), (1, 2, 11), (0, 2, 13), (1, 5, 1), (0, 5, 8), (0, 5, 9),
+    (1, 4, 0), (0, 4, 7), (1, 3, 6), (0, 4, 4), (0, 5, 5), (0, 4, 6), (1, 0, 13), (3, 1, 0), (3, 1, 1), (4, 1, 0),
+    (4, 1, 32), (2, 1, 0), (4, 0, 16), (4, 0, 48), (1, 2, 10), (1, 3, 11), (0, 3, 13), (1, 4, 1), (0, 4, 8),
+    (0, 4, 5), (0, 4, 9), (1, 5, 0), (0, 5, 4), (0, 5, 7), (0, 5, 6), (1, 3, 10), (1, 2, 13), (1, 4, 12),
+    (0, 4, 15), (0, 4, 14), (1, 3, 15), (1, 3, 14), (3, 2, 0), (3, 2, 1), (4, 2, 0), (4, 2, 32), (1, 5, 9),
+    (1, 5, 8), (1, 4, 7), (4, 1, 8), (4, 1, 40), (1, 4, 6), (1, 5, 15), (1, 5, 14), (1, 3, 13), (3, 3, 0),
+    (4, 0, 24), (3, 3, 1), (4, 3, 0), (4, 3, 32), (2, 2, 0), (1, 4, 8), (1, 5, 5), (1, 4, 4), (1, 4, 9), (1, 5, 6),
+    (1, 4, 5), (0, 4, 10), (0, 4, 11), (1, 5, 4), (0, 5, 11), (0, 5, 10), (1, 5, 7), (4, 2, 8), (4, 2, 40),
+    (4, 1, 48), (4, 1, 16), (1, 4, 15), (1, 4, 14), (3, 4, 0), (3, 4, 1), (4, 4, 0), (4, 4, 32), (4, 3, 8),
+    (5, 0, 0), (4, 3, 40), (1, 4, 10), (1, 4, 11), (0, 4, 13), (4, 2, 48), (4, 2, 16), (1, 5, 10), (1, 5, 11),
+    (0, 5, 13), (4, 1, 24), (4, 4, 8), (4, 4, 40), (1, 4, 13), (4, 3, 48), (4, 3, 16), (1, 5, 13), (3, 5, 0),
+    (4, 2, 24), (4, 5, 0), (4, 5, 8), (4, 5, 16), (4, 5, 24), (4, 5, 32), (3, 5, 1), (4, 5, 1), (4, 5, 9),
+    (4, 5, 17), (4, 5, 25), (4, 4, 16), (4, 5, 33), (5, 1, 0), (4, 4, 48), (4, 3, 24), (4, 5, 48), (5, 2, 0),
+    (4, 5, 40), (4, 5, 41), (4, 5, 49), (4, 4, 24), (5, 3, 0), (5, 5, 0), (5, 5, 1), (5, 4, 0),
 )
 
 
@@ -174,21 +172,19 @@
         odd = lax.rem(z + 1 + unit % 2, 2)
         return pl.ds(pl.multiple_of(row_at(owner) * OWN + odd * HALF, HALF), HALF)
 
-    def multiply(unit, tile):
+    def multiply(unit, part):
         k = unit // 2
-        each = 8 // TILES[unit]
-        owners = OWNERS[unit][tile * each : (tile + 1) * each]
         lines = []
-        for owner in owners:
+        for owner in range(NY):
             rows = spread(unit, owner)
             lines.append(jnp.concatenate([gathered[k, 0, rows, :], gathered[k, 1, rows, :]], axis=1))
-        both = jnp.concatenate(lines, axis=0)
-        for part in range(2):
-            value = lax.dot_general(
-                both, factor[k, part], (((1,), (1,)), ((), ())), preferred_element_type=jnp.float32
-            )
-            for i, owner in enumerate(owners):
-                product[unit, part, owner % 8] = value[i * HALF : (i + 1) * HALF]
+        value = lax.dot_general(
+            jnp.concatenate(lines, axis=0),
+            factor[k, part],
+            (((1,), (1,)), ((), ())),
+            preferred_element_type=jnp.float32,
+        )
+        product[unit, part] = value.reshape(NY, HALF, TILE)
 
     def way(unit, slot, sub):
         turn = 1 if (sub if unit == LAST else unit) % 2 == 0 else -1
@@ -281,12 +277,23 @@
     density_ref[...] = total[:, :PIECE]
 
 
+def hand_over(panel_ref, density_ref, panel_out, density_out, sem):
+    copies = [
+        pltpu.make_async_copy(panel_ref, panel_out, sem.at[0]),
+        pltpu.make_async_copy(density_ref, density_out, sem.at[1]),
+    ]
+    for copy in copies:
+        copy.start()
+    for copy in copies:
+        copy.wait()
+
+
 def body(inverse, lower, mask_tiles, pole_weight):
     anywhere = pl.BlockSpec(memory_space=pl.ANY)
     vmem = pl.BlockSpec(memory_space=pltpu.VMEM)
     smem = pl.BlockSpec(memory_space=pltpu.SMEM)
     bf16, f32 = jnp.bfloat16, jnp.float32
-    panel, density = pl.pallas_call(
+    arrays = pl.pallas_call(
         kernel,
         out_shape=(
             jax.ShapeDtypeStruct((KP, 2, OWN, TILE), bf16),
@@ -320,6 +327,14 @@
         ),
         name="panel_update",
     )(inverse, jnp.swapaxes(lower, 2, 3), mask_tiles, jnp.swapaxes(pole_weight, 0, 1))
+    panel, density = pl.pallas_call(
+        hand_over,
+        out_shape=tuple(jax.ShapeDtypeStruct(array.shape, array.dtype) for array in arrays),
+        in_specs=[vmem, vmem],
+        out_specs=(anywhere, anywhere),
+        scratch_shapes=[pltpu.SemaphoreType.DMA((2,))],
+        name="hand_over",
+    )(*arrays)
     return jnp.swapaxes(panel, 2, 3), jnp.swapaxes(density, 0, 1)
 
 

time: 80.4 us -> 78.4 us (0.975)
  local copies, waits for them, and re-layouts: 3.08 us -> 0 us
  Pallas kernels: 76.4 us -> 77.4 us
    unnamed x2 -> x0, local copies, waits for them, and re-layouts: 3.08 us -> none
    pallas_call x0 -> x1, Pallas kernels: none -> 1.7 us  [body(): pl.pallas_call(hand_over, out_shape=tuple((jax.ShapeDtypeStruct(array.sha...]
where the time goes in v4:
time: 78.4 us; the launch traced here: 78 us
  Pallas kernels  77.4 us (99%)
    pallas_call x1, Pallas kernels, body(): pl.pallas_call(kernel, out_shape=(jax.ShapeDtypeStruct((KP, 2, OWN, TILE)...  75.7 us
    pallas_call x1, Pallas kernels, body(): pl.pallas_call(hand_over, out_shape=tuple((jax.ShapeDtypeStruct(array.sha...  1.7 us

profile of v4, /device:TPU:1, one launch (start us, length us, event | category | flops | bytes accessed | tf_op | source)
XLA Modules:
  0.0 78.0 jit_solution(12262848203063412115)
XLA Ops:
  0.6 75.7 %panel_update.1 = (bf16[3,2,64,384]{3,2,1,0:T(8,128)(2,1)}, f32[64,96]{1,0:T(8,128)}) custom-call(bf16[3,2,384,768]{3,2,1,0:T(8,128)(2,1)} %inverse_ref.1, bf16[3,2,32,768]{3,2,1,0:T(8,128)(2,1)} %bitcast.4, s32[16,16]{1,0:T(8,128)} %mask_ref.1, f32[2,3]{1,0:T(2,128)} %bitcast.5), custom_call_target="tpu_custom_call" | custom-call | tf_op jit(solution)/shard_map/panel_update/pallas_call | solution.py:296
  76.3 1.7 %hand_over.1 = (bf16[3,2,64,384]{3,2,1,0:T(8,128)(2,1)}, f32[64,96]{1,0:T(8,128)}) custom-call(bf16[3,2,64,384]{3,2,1,0:T(8,128)(2,1)} %get-tuple-element.6.panel_ref, f32[64,96]{1,0:T(8,128)} %get-tuple-element.7.density_ref), custom_call_target="tpu_custom_call" | custom-call | tf_op jit(solution)/shard_map/hand_over/pallas_call | solution.py:330

commit v5 on v4

--- a/solution.py
+++ b/solution.py
@@ -108,9 +108,6 @@
     ]
     first_own = pl.multiple_of(place(0, 0) * WIDE, WIDE)
     own = pltpu.make_async_copy(lower_ref, gathered.at[:, :, pl.ds(first_own, WIDE), :], own_sem)
-    own.start()
-    for load in loads:
-        load.start()
 
     barrier = pltpu.get_barrier_semaphore()
     for step in (("x", 1), ("x", -1), ("z", 1), ("z", -1)):
@@ -119,6 +116,9 @@
         pl.semaphore_signal(barrier, inc=1, device_id={"row": row_at(by)}, device_id_type=MESH)
     for by in (1, 2, 3):
         pl.semaphore_signal(barrier, inc=1, device_id={"pole": pole_at(by)}, device_id_type=MESH)
+    own.start()
+    for load in loads:
+        load.start()
     pl.semaphore_wait(barrier, 11)
 
     def spot(slab, chunk, rows):

time: 78.4 us -> 78.4 us (level)
  no operation moved by 1% of the time
where the time goes in v5:
time: 78.4 us; the launch traced here: 78 us
  Pallas kernels  77.4 us (99%)
    pallas_call x1, Pallas kernels, body(): pl.pallas_call(kernel, out_shape=(jax.ShapeDtypeStruct((KP, 2, OWN, TILE)...  75.7 us
    pallas_call x1, Pallas kernels, body(): pl.pallas_call(hand_over, out_shape=tuple((jax.ShapeDtypeStruct(array.sha...  1.7 us

profile of v5, /device:TPU:1, one launch (start us, length us, event | category | flops | bytes accessed | tf_op | source)
XLA Modules:
  0.0 78.0 jit_solution(5441225959439038564)
XLA Ops:
  0.6 75.7 %panel_update.1 = (bf16[3,2,64,384]{3,2,1,0:T(8,128)(2,1)}, f32[64,96]{1,0:T(8,128)}) custom-call(bf16[3,2,384,768]{3,2,1,0:T(8,128)(2,1)} %inverse_ref.1, bf16[3,2,32,768]{3,2,1,0:T(8,128)(2,1)} %bitcast.4, s32[16,16]{1,0:T(8,128)} %mask_ref.1, f32[2,3]{1,0:T(2,128)} %bitcast.5), custom_call_target="tpu_custom_call" | custom-call | tf_op jit(solution)/shard_map/panel_update/pallas_call | solution.py:296
  76.3 1.7 %hand_over.1 = (bf16[3,2,64,384]{3,2,1,0:T(8,128)(2,1)}, f32[64,96]{1,0:T(8,128)}) custom-call(bf16[3,2,64,384]{3,2,1,0:T(8,128)(2,1)} %get-tuple-element.6.panel_ref, f32[64,96]{1,0:T(8,128)} %get-tuple-element.7.density_ref), custom_call_target="tpu_custom_call" | custom-call | tf_op jit(solution)/shard_map/hand_over/pallas_call | solution.py:330
